TPU v7x, 512 devices: a whole 4x4x16 slice. The times are simulated.
512 devices in a mesh: dp: 32 (over x_lo, z), seq: 4 (over y), mp: 4 (over x_hi, core).
Axes of the slice: x: 4 (x_hi: 2, x_lo: 2; x = x_hi * 2 + x_lo), y: 4, z: 16, core: 2. Of those that a mesh axis runs over, the one named last changes fastest.
Arguments:
- hidden: bfloat16 [32768, 6656], P(('dp', 'seq'), 'mp'), may hold values from -6 to 6
- cotangent: bfloat16 [32768, 17920], P(('dp', 'seq'), 'mp'), may hold values from -6 to 6
- frozen_down: bfloat16 [6656, 4], P('mp'), may hold values from -0.078125 to 0.078125
- adapter: float32 [4, 4, 4480], P('mp', None, ('dp', 'seq')), may hold values from -6 to 6
- prior: float32 [48], replicated, may hold values from 0.2 to 5
- domain_of: int32 [64], P('dp'), may hold values from 0 to 47
Outputs:
- new_adapter: float32 [4, 4, 4480], P('mp', None, ('dp', 'seq'))
- log_weights: float32 [48], replicated
All inputs are finite; a program needn't handle non-finite values.
Results may differ from a plain program's by a relative error of at most 0.014.
Values may be sent and summed in bfloat16 or wider, within the bound.
A program may use at most 64 MiB of HBM per device.

v0:
```python
import jax
import jax.numpy as jnp
from jax import lax
from jax.sharding import PartitionSpec as P

FF = 17920
NDOM = 48
RANK = 4


step_rate = 1.0
learn_rate = 0.5


def expand_weights(weights):
    return (weights[:, None, None] * jnp.eye(RANK, dtype=jnp.float32)[None, :, :]).reshape(
        NDOM * RANK, RANK
    )


def domain_scores(terms, mixture):
    return jnp.sum(terms.reshape(terms.shape[0], NDOM, RANK) * mixture[:, None, :], axis=(0, 2))


def reweight(weights, scores, sumsq):
    meansq = sumsq / (RANK * FF) + 1e-06
    ratio = scores / (RANK * FF * meansq)
    raised = weights * jnp.exp(step_rate * ratio)
    log_new = jnp.log(weights) + step_rate * ratio - jnp.log(jnp.sum(raised))
    return (log_new, meansq)


def body(hidden, cotangent, frozen_down, adapter, prior, domain_of):
    rows = hidden.shape[0]
    piece = rows // domain_of.shape[0]
    partial_down = jnp.dot(hidden, frozen_down, preferred_element_type=jnp.float32)
    down = lax.psum(partial_down.astype(jnp.bfloat16), "mp")
    domain_tok = jnp.repeat(domain_of, piece, total_repeat_length=rows)
    onehot = (domain_tok[:, None] == jnp.arange(NDOM, dtype=jnp.int32)[None, :]).astype(
        jnp.bfloat16
    )
    spread = (onehot[:, :, None] * down[:, None, :]).reshape(rows, NDOM * RANK)
    weights = prior / jnp.sum(prior)
    highest = lax.Precision.HIGHEST
    shard = lax.psum_scatter(
        lax.dot_general(
            cotangent, spread, (((0,), (0,)), ((), ())), preferred_element_type=jnp.float32
        ),
        ("dp", "seq"),
        scatter_dimension=0,
        tiled=True,
    )
    mixture = jnp.dot(shard, expand_weights(weights), precision=highest)
    scores, sumsq = lax.psum(
        (domain_scores(shard, mixture), jnp.sum(mixture * mixture)), ("dp", "seq", "mp")
    )
    log_new, meansq = reweight(weights, scores, sumsq)
    update = jnp.dot(shard, expand_weights(jnp.exp(log_new)), precision=highest)
    new_adapter = adapter - learn_rate * update.T[None, :, :] / jnp.sqrt(meansq)
    return (new_adapter, log_new)


def solution(mesh):
    return jax.shard_map(
        body,
        mesh=mesh,
        in_specs=(
            P(("dp", "seq"), "mp"),
            P(("dp", "seq"), "mp"),
            P("mp", None),
            P("mp", None, ("dp", "seq")),
            P(),
            P("dp"),
        ),
        out_specs=(P("mp", None, ("dp", "seq")), P()),
        check_vma=False,
    )
```

profile of v0, /device:TPU:1, one launch (start us, length us, event | category | flops | bytes accessed | tf_op | source)
XLA Modules:
  0.0 1317.5 jit_solution(4457269442039612143)
XLA Ops:
  7.2 0.0 copy-start
  7.2 0.0 all-reduce.4.cloned.1.call-start
  7.2 1.4 fusion.17
  8.7 1.3 compare_select_fusion.1
  10.0 1.4 convolution_convert_fusion
  11.4 13.4 %psum.21 = bf16[256,4]{0,1:T(4,128)(2,1)S(1)} all-reduce(bf16[256,4]{0,1:T(4,128)(2,1)S(1)} %convolution_convert_fusion), channel_id=1, replica_groups=mesh['dp'=32,'seq'=4,'mp'=4] {'mp'}, use_global_device_ids=true, to_apply=%region_1.2 | all-reduce | flops 1024 | bytes 4096 | tf_op jit(solution)/shard_map/psum | solution.py:37
  24.9 0.1 broadcast_multiply_fusion
  25.0 0.0 copy-done
  25.0 2.4 convolution_bitcast_fusion
  27.4 0.0 copy-start.2
  27.4 0.0 copy-start.1
  27.4 0.0 all-reduce.4.cloned.1.call-update
  27.4 0.6 copy-done.2
  28.0 0.6 reduce_sum.43
  28.6 0.6 broadcast_divide_fusion.1
  29.3 0.1 mul.88
  29.4 0.1 mul.89
  29.5 1.3 dynamic-slice.6
  31.4 1092.8 %all-reduce.4.cloned.1.call-done = f32[4480,192]{0,1:T(8,128)} async-done(((f32[4480,192]{0,1:T(8,128)}), f32[4480,192]{0,1:T(8,128)}) %all-reduce.4.cloned.1.call-update) | async-done | bytes 3440656
  1124.3 1.9 multiply_reduce_fusion.1
  1126.2 1.1 multiply_reduce_fusion
  1127.3 0.1 reduce_sum.45
  1127.5 0.1 reduce_sum.46
  1127.6 177.2 %all-reduce.1 = (f32[48]{0:T(128)S(1)}, f32[]{:T(128)}) all-reduce(f32[48]{0:T(128)S(1)} %reduce_sum.46, f32[]{:T(128)} %get-tuple-element.22), channel_id=1, replica_groups=mesh['dp'=32,'seq'=4,'mp'=4] {'dp','seq','mp'}, use_global_device_ids=true, to_apply=%region_5.6 | all-reduce | flops 49 | bytes 392 | tf_op jit(solution)/shard_map/psum | solution.py:54
  1305.4 1.3 multiply_reduce_fusion.2
  1307.4 1.2 fusion.16
  1308.6 0.1 mul.100
  1308.6 0.1 mul.101
  1308.8 0.0 copy-done.1
  1308.8 1.9 fusion.2
  (8 shorter events, 0.1 us)
Async XLA Ops:
  7.2 17.8 %copy-start = (bf16[256,4480]{1,0:T(8,128)(2,1)S(1)}, bf16[256,4480]{1,0:T(8,128)(2,1)}, u32[]{:S(2)}) copy-start(bf16[256,4480]{1,0:T(8,128)(2,1)} %param.9) | copy-start | bytes 6881284
  7.2 1117.1 %all-reduce.4.cloned.1.call-start = ((), (), s32[]{:S(2)}) async-start(), calls=%async_computation | async-start | bytes 6881280
  27.4 0.7 copy-start.2
  27.4 1281.4 %copy-start.1 = (f32[1,4,35]{2,1,0:T(4,128)S(1)}, f32[1,4,35]{2,1,0:T(4,128)}, u32[]{:S(2)}) copy-start(f32[1,4,35]{2,1,0:T(4,128)} %param.11) | copy-start | bytes 1684
Sparse Core Ops, SparseCore 0:
  27.5 1096.6 all-reduce.3
where the time goes:
time: 1320 us
  waiting for transfers between devices  1090 us (83%)
  blocking collectives  191 us (14%)
  between operations  16.2 us (1%)
    unnamed x2, waiting for transfers between devices  1090 us
    psum x1, blocking collectives, body(): lax.psum((domain_scores(shard, mixture), jnp.sum(mixture * mixture)), ('d...  177 us
  transfers between devices with their start and end apart: 1, of which 1 were waited for; matrix products, arithmetic and copies ran while one was open for 0% of the time, Pallas kernels for 0%

commit v1 on v0

v1 whole, which is shorter than its diff:
```python
import functools

import jax
import jax.numpy as jnp
from jax import lax
from jax.experimental import pallas as pl
from jax.experimental.pallas import tpu as pltpu
from jax.sharding import PartitionSpec as P

FF = 17920
NDOM = 48
RANK = 4
ROWS = 256
PIECE = 128
DM = 1664
FFM = 4480
N_DP = 32
N_SEQ = 4
N_MP = 4
COLS = FFM // (N_DP * N_SEQ)
LANES = 128
HALF = 64
CHUNKS = 7
WIDTH = FFM // CHUNKS

SEND = jnp.bfloat16
MESH = pl.DeviceIdType.MESH
step_rate = 1.0
learn_rate = 0.5


def kernel(
    hid_hbm, cot_hbm, fro_hbm, ada_hbm, pri_hbm, dom_hbm,
    out_ref, log_ref,
    hid, cot, fro, ada, pri, dom, wrow, part, lhs, g, spread, seqbuf, total, got, gotf, rows_a, rows_b,
    in_sem, cot_sem, small_sem, s1, r1, s2, r2, s3, r3, s4, r4, s5, r5,
):
    dp, seq, mp = lax.axis_index("dp"), lax.axis_index("seq"), lax.axis_index("mp")

    def to(d=0, s=0, m=0):
        return {
            "dp": lax.rem(dp + d, N_DP),
            "seq": lax.rem(seq + s, N_SEQ),
            "mp": lax.rem(mp + m, N_MP),
        }

    def send(src, dst, ssem, rsem, **where):
        copy = pltpu.make_async_remote_copy(
            src_ref=src, dst_ref=dst, send_sem=ssem, recv_sem=rsem,
            device_id=to(**where), device_id_type=MESH,
        )
        copy.start()

    def done(ref, ssem, rsem, **where):
        return pltpu.make_async_remote_copy(
            src_ref=ref, dst_ref=ref, send_sem=ssem, recv_sem=rsem,
            device_id=to(**where), device_id_type=MESH,
        )

    barrier = pltpu.get_barrier_semaphore()
    plane = [(s, m) for s in range(N_SEQ) for m in range(N_MP) if (s, m) != (0, 0)]
    for s, m in plane:
        pl.semaphore_signal(barrier, inc=1, device_id=to(s=s, m=m), device_id_type=MESH)
    for j in range(1, N_DP):
        pl.semaphore_signal(barrier, inc=1, device_id=to(d=j), device_id_type=MESH)

    loads = [
        pltpu.make_async_copy(fro_hbm, fro, in_sem.at[0]),
        pltpu.make_async_copy(hid_hbm, hid, in_sem.at[1]),
    ]
    for load in loads:
        load.start()
    cot_loads = []
    for c in range(CHUNKS):
        cut = pl.ds(c * WIDTH, WIDTH)
        load = pltpu.make_async_copy(cot_hbm.at[:, cut], cot.at[:, cut], cot_sem.at[c])
        load.start()
        cot_loads.append(load)
    small = [
        pltpu.make_async_copy(ada_hbm, ada, small_sem.at[0]),
        pltpu.make_async_copy(pri_hbm, pri, small_sem.at[1]),
        pltpu.make_async_copy(dom_hbm, dom, small_sem.at[2]),
    ]
    for load in small:
        load.start()

    lhs[...] = jnp.zeros_like(lhs)
    wrow[...] = jnp.zeros_like(wrow)

    for load in loads:
        load.wait()
    partial = lax.dot_general(
        fro[...], hid[...], (((1,), (1,)), ((), ())), preferred_element_type=jnp.float32
    )
    part[0] = partial.astype(jnp.bfloat16).astype(jnp.float32)

    pl.semaphore_wait(barrier, len(plane) + N_DP - 1)

    for m in range(1, N_MP):
        send(part.at[0], part.at[m], s1, r1, m=m)
    done(part.at[pl.ds(1, N_MP - 1)], s1, r1, m=1).wait_recv()
    down = part[0] + part[1] + part[2] + part[3]
    token = lax.broadcasted_iota(jnp.int32, (RANK, ROWS), 1)
    lhs[0:RANK] = jnp.where(token < PIECE, down, 0.0)
    lhs[8 : 8 + RANK] = jnp.where(token < PIECE, 0.0, down)
    left = lhs[...].astype(jnp.bfloat16)
    for c in range(CHUNKS):
        cut = slice(c * WIDTH, (c + 1) * WIDTH)
        cot_loads[c].wait()
        g[:, cut] = jnp.dot(left, cot[:, cut], preferred_element_type=jnp.float32)

    lane = lax.broadcasted_iota(jnp.int32, (8, LANES), 1)
    for p in range(N_DP * N_SEQ):
        v, o = divmod(p * COLS, LANES)
        a = g[0:8, v * LANES : (v + 1) * LANES]
        b = g[8:16, v * LANES : (v + 1) * LANES]
        a = a if o == 0 else pltpu.roll(a, LANES - o, 1)
        b = pltpu.roll(b, (HALF - o) % LANES, 1) if o != HALF else b
        if o + COLS > LANES:
            a2 = g[0:8, (v + 1) * LANES : (v + 2) * LANES]
            b2 = g[8:16, (v + 1) * LANES : (v + 2) * LANES]
            a2 = pltpu.roll(a2, LANES - o, 1)
            b2 = pltpu.roll(b2, (HALF - o) % LANES, 1) if o != HALF else b2
            a = jnp.where(lane < LANES - o, a, a2)
            b = jnp.where(lane < HALF + LANES - o, b, b2)
        joined = jnp.where(lane < HALF, a, b)
        spread[p % N_SEQ, p // N_SEQ] = joined[0:RANK].astype(SEND)

    for s in range(1, N_SEQ):
        send(spread.at[lax.rem(seq + s, N_SEQ)], seqbuf.at[s - 1], s2, r2, s=s)
    for load in small:
        load.wait()
    d0 = dom[0].astype(jnp.float32)
    d1 = dom[1].astype(jnp.float32)
    done(seqbuf, s2, r2, s=1).wait_recv()
    f32 = jnp.float32
    summed = (
        spread[seq].astype(f32) + seqbuf[0].astype(f32) + seqbuf[1].astype(f32) + seqbuf[2].astype(f32)
    )
    lane3 = lax.broadcasted_iota(jnp.int32, (N_DP, RANK, LANES), 2)
    summed = jnp.where(lane3 == COLS, d0, jnp.where(lane3 == HALF + COLS, d1, summed))
    total[...] = summed.astype(SEND)

    for j in range(1, N_DP):
        send(total.at[lax.rem(dp + j, N_DP)], got.at[j], s3, r3, d=j)
    got[0] = total[dp]

    wrow[:, 0:NDOM] = pri[...]
    prior = wrow[...]
    weights = prior / jnp.sum(prior, axis=1, keepdims=True)
    lane1 = lax.broadcasted_iota(jnp.int32, (1, LANES), 1)
    lane2 = lax.broadcasted_iota(jnp.int32, (N_DP, LANES), 1)
    low = lane2 < HALF

    done(got.at[pl.ds(1, N_DP - 1)], s3, r3, d=1).wait_recv()
    gotf[...] = got[...].astype(f32)
    rank_rows = [gotf[:, r, :] for r in range(RANK)]
    dom0 = jnp.sum(jnp.where(lane2 == COLS, rank_rows[0], 0.0), axis=1, keepdims=True)
    dom1 = jnp.sum(jnp.where(lane2 == HALF + COLS, rank_rows[0], 0.0), axis=1, keepdims=True)
    lanef = lane2.astype(f32)
    hot0 = (lanef == dom0).astype(f32)
    hot1 = (lanef == dom1).astype(f32)

    def per_sequence(row):
        return jnp.where(
            low,
            jnp.sum(hot0 * row, axis=1, keepdims=True),
            jnp.sum(hot1 * row, axis=1, keepdims=True),
        )

    def combine(scale):
        sums = [jnp.sum(scale * x, axis=0, keepdims=True) for x in rank_rows]
        return [x + pltpu.roll(x, HALF, 1) for x in sums]

    valid = (lane1 < COLS) | ((lane1 >= HALF) & (lane1 < HALF + COLS))
    mixture = [jnp.where(valid, x, 0.0) for x in combine(per_sequence(weights))]
    square = sum(x * x for x in mixture)
    sumsq = jnp.sum(jnp.where(lane1 < HALF, square, 0.0), axis=1, keepdims=True)
    product = sum(x * y for x, y in zip(rank_rows, mixture))
    score0 = jnp.sum(jnp.where(low, product, 0.0), axis=1, keepdims=True)
    score1 = jnp.sum(jnp.where(low, 0.0, product), axis=1, keepdims=True)
    row = jnp.sum(hot0 * score0 + hot1 * score1, axis=0, keepdims=True)
    row = jnp.where(lane1 == LANES - 1, sumsq, row)

    mine = seq * N_MP + mp
    rows_a[mine] = row
    for s, m in plane:
        send(rows_a.at[mine], rows_a.at[mine], s4, r4, s=s, m=m)
    done(rows_a.at[pl.ds(0, len(plane))], s4, r4, s=1).wait_recv()
    row = jnp.sum(rows_a[...], axis=0)
    rows_b[dp] = row
    for j in range(1, N_DP):
        send(rows_b.at[dp], rows_b.at[dp], s5, r5, d=j)
    done(rows_b.at[pl.ds(0, N_DP - 1)], s5, r5, d=1).wait_recv()
    row = jnp.sum(rows_b[...], axis=0)

    sumsq = jnp.sum(jnp.where(lane1 == LANES - 1, row, 0.0), axis=1, keepdims=True)
    scores = jnp.where(lane1 < NDOM, row, 0.0)
    meansq = sumsq / (RANK * FF) + 1e-06
    ratio = scores / (RANK * FF * meansq)
    raised = weights * jnp.exp(step_rate * ratio)
    log_new = jnp.log(weights) + step_rate * ratio - jnp.log(jnp.sum(raised, axis=1, keepdims=True))
    log_ref[...] = log_new[:, 0:NDOM]
    new = jnp.where(lane1 < NDOM, jnp.exp(log_new), 0.0)
    update = combine(per_sequence(new))
    root = jnp.sqrt(meansq)
    for r in range(RANK):
        moved = learn_rate * update[r] / root
        out_ref[r : r + 1, :] = ada[r : r + 1, :] - moved[:, 0:COLS]

    done(part.at[pl.ds(1, N_MP - 1)], s1, r1, m=1).wait_send()
    done(seqbuf, s2, r2, s=1).wait_send()
    done(got.at[pl.ds(1, N_DP - 1)], s3, r3, d=1).wait_send()
    done(rows_a.at[pl.ds(0, len(plane))], s4, r4, s=1).wait_send()
    done(rows_b.at[pl.ds(0, N_DP - 1)], s5, r5, d=1).wait_send()


def body(hidden, cotangent, frozen_down, adapter, prior, domain_of):
    f32 = jnp.float32
    sem = pltpu.SemaphoreType.DMA
    out, log_new = pl.pallas_call(
        kernel,
        out_shape=(
            jax.ShapeDtypeStruct((RANK, COLS), f32),
            jax.ShapeDtypeStruct((1, NDOM), f32),
        ),
        in_specs=[pl.BlockSpec(memory_space=pl.ANY)] * 6,
        out_specs=(pl.BlockSpec(memory_space=pltpu.VMEM),) * 2,
        scratch_shapes=[
            pltpu.VMEM((ROWS, DM), jnp.bfloat16),
            pltpu.VMEM((ROWS, FFM), jnp.bfloat16),
            pltpu.VMEM((RANK, DM), jnp.bfloat16),
            pltpu.VMEM((RANK, COLS), f32),
            pltpu.VMEM((1, NDOM), f32),
            pltpu.SMEM((2,), jnp.int32),
            pltpu.VMEM((1, LANES), f32),
            pltpu.VMEM((N_MP, RANK, ROWS), f32),
            pltpu.VMEM((16, ROWS), f32),
            pltpu.VMEM((16, FFM), f32),
            pltpu.VMEM((N_SEQ, N_DP, RANK, LANES), SEND),
            pltpu.VMEM((N_SEQ - 1, N_DP, RANK, LANES), SEND),
            pltpu.VMEM((N_DP, RANK, LANES), SEND),
            pltpu.VMEM((N_DP, RANK, LANES), SEND),
            pltpu.VMEM((N_DP, RANK, LANES), f32),
            pltpu.VMEM((N_SEQ * N_MP, 1, LANES), f32),
            pltpu.VMEM((N_DP, 1, LANES), f32),
            sem((2,)),
            sem((CHUNKS,)),
            sem((3,)),
        ]
        + [sem] * 10,
        compiler_params=pltpu.CompilerParams(
            collective_id=0, has_side_effects=True, vmem_limit_bytes=60 << 20
        ),
    )(hidden, cotangent, frozen_down.T, adapter.reshape(RANK, COLS), prior.reshape(1, NDOM), domain_of)
    return out.reshape(1, RANK, COLS), log_new.reshape(NDOM)


def solution(mesh):
    return jax.shard_map(
        body,
        mesh=mesh,
        in_specs=(
            P(("dp", "seq"), "mp"),
            P(("dp", "seq"), "mp"),
            P("mp", None),
            P("mp", None, ("dp", "seq")),
            P(),
            P("dp"),
        ),
        out_specs=(P("mp", None, ("dp", "seq")), P()),
        check_vma=False,
    )
```

time: 1320 us -> 50.4 us (0.04)
  waiting for transfers between devices: 1090 us -> 0 us
  blocking collectives: 191 us -> 0 us
  Pallas kernels: 0 us -> 47.2 us
  between operations: 16.2 us -> 0.64 us
    unnamed x2 -> x0, waiting for transfers between devices: 1090 us -> none
    psum x2 -> x0, blocking collectives: 191 us -> none  [the longest x1 177 us: body(): lax.psum((domain_scores(shard, mixture), jnp.sum(mixture * mixture)), ('d...]
    pallas_call x0 -> x1, Pallas kernels: none -> 47.2 us  [body(): pl.pallas_call(kernel, out_shape=(jax.ShapeDtypeStruct((RANK, COLS), f32)...]
  transfers between devices with their start and end apart: 1 -> 0, of which waited for: 1 -> 0; matrix products, arithmetic and copies ran while one was open for 0% -> 0% of each run, Pallas kernels for 0% -> 0%
where the time goes in v1:
time: 50.4 us; the launch traced here: 50.2 us
  Pallas kernels  47.2 us (94%)
  local copies, waits for them, and re-layouts  2.39 us (5%)
  between operations  0.64 us (1%)
    pallas_call x1, Pallas kernels, body(): pl.pallas_call(kernel, out_shape=(jax.ShapeDtypeStruct((RANK, COLS), f32)...  47.2 us
    unnamed x2, local copies, waits for them, and re-layouts  2.39 us

profile of v1, /device:TPU:1, one launch (start us, length us, event | category | flops | bytes accessed | tf_op | source)
XLA Modules:
  0.0 50.2 jit_solution(16460114780739689389)
XLA Ops:
  0.6 47.2 %shard_map.77 = (f32[4,35]{1,0:T(4,128)}, f32[1,48]{1,0:T(1,128)}) custom-call(bf16[256,1664]{1,0:T(8,128)(2,1)} %hid_hbm.1, bf16[256,4480]{1,0:T(8,128)(2,1)} %cot_hbm.1, bf16[4,1664]{1,0:T(4,128)(2,1)} %bitcast.5, f32[4,35]{1,0:T(4,128)} %bitcast.6, f32[1,48]{1,0:T(1,128)} %bitcast.8, s32[2]{0:T(128)} %dom_hbm.1), custom_call_target="tpu_custom_call" | custom-call | tf_op jit(solution)/shard_map/pallas_call | solution.py:221
  47.8 1.2 %copy.10 = f32[1,4,35]{2,1,0:T(4,128)} copy(f32[1,4,35]{2,1,0:T(4,128)} %bitcast.7) | data formatting | bytes 1120
  49.1 1.1 %copy.11 = f32[48]{0:T(128)} copy(f32[48]{0:T(128)} %bitcast.9) | data formatting | bytes 384

commit v2 on v1

--- a/solution.py
+++ b/solution.py
@@ -24,6 +24,8 @@
 WIDTH = FFM // CHUNKS
 
 SEND = jnp.bfloat16
+N_Z = 16
+ORDER = (0, 1, 2, 3, 4, 5, 6, 7, 15, 8, 14, 9, 13, 10, 12, 11)
 MESH = pl.DeviceIdType.MESH
 step_rate = 1.0
 learn_rate = 0.5
@@ -33,7 +35,7 @@
     hid_hbm, cot_hbm, fro_hbm, ada_hbm, pri_hbm, dom_hbm,
     out_ref, log_ref,
     hid, cot, fro, ada, pri, dom, wrow, part, lhs, g, spread, seqbuf, total, got, gotf, rows_a, rows_b,
-    in_sem, cot_sem, small_sem, s1, r1, s2, r2, s3, r3, s4, r4, s5, r5,
+    in_sem, cot_sem, small_sem, s1, r1, s2, r2, s3, r3, s4, r4, s5, r5, ready,
 ):
     dp, seq, mp = lax.axis_index("dp"), lax.axis_index("seq"), lax.axis_index("mp")
 
@@ -44,10 +46,16 @@
             "mp": lax.rem(mp + m, N_MP),
         }
 
-    def send(src, dst, ssem, rsem, **where):
+    z = lax.rem(dp, N_Z)
+    place = jnp.where(z < 8, z, jnp.where(z < 12, 2 * z - 7, 38 - 2 * z))
+
+    def at(d):
+        return {"dp": d, "seq": seq, "mp": mp}
+
+    def send(src, dst, ssem, rsem, target=None, **where):
         copy = pltpu.make_async_remote_copy(
             src_ref=src, dst_ref=dst, send_sem=ssem, recv_sem=rsem,
-            device_id=to(**where), device_id_type=MESH,
+            device_id=to(**where) if target is None else target, device_id_type=MESH,
         )
         copy.start()
 
@@ -61,8 +69,14 @@
     plane = [(s, m) for s in range(N_SEQ) for m in range(N_MP) if (s, m) != (0, 0)]
     for s, m in plane:
         pl.semaphore_signal(barrier, inc=1, device_id=to(s=s, m=m), device_id_type=MESH)
-    for j in range(1, N_DP):
-        pl.semaphore_signal(barrier, inc=1, device_id=to(d=j), device_id_type=MESH)
+    pl.semaphore_signal(barrier, inc=1, device_id=to(d=N_Z), device_id_type=MESH)
+    for position, plane_z in enumerate(ORDER):
+
+        @pl.when(place < position)
+        def _():
+            for x in range(2):
+                pl.semaphore_signal(barrier, inc=1, device_id=at(x * N_Z + plane_z), device_id_type=MESH)
+
 
     loads = [
         pltpu.make_async_copy(fro_hbm, fro, in_sem.at[0]),
@@ -94,7 +108,15 @@
     )
     part[0] = partial.astype(jnp.bfloat16).astype(jnp.float32)
 
-    pl.semaphore_wait(barrier, len(plane) + N_DP - 1)
+    pl.semaphore_wait(barrier, len(plane) + 1 + 2 * place)
+    for position, plane_z in enumerate(ORDER):
+
+        @pl.when(place > position)
+        def _():
+            for x in range(2):
+                pl.semaphore_signal(
+                    ready.at[z], inc=1, device_id=at(x * N_Z + plane_z), device_id_type=MESH
+                )
 
     for m in range(1, N_MP):
         send(part.at[0], part.at[m], s1, r1, m=m)
@@ -141,9 +163,21 @@
     summed = jnp.where(lane3 == COLS, d0, jnp.where(lane3 == HALF + COLS, d1, summed))
     total[...] = summed.astype(SEND)
 
-    for j in range(1, N_DP):
-        send(total.at[lax.rem(dp + j, N_DP)], got.at[j], s3, r3, d=j)
-    got[0] = total[dp]
+    partner = lax.rem(dp + N_Z, N_DP)
+    send(total.at[partner], got.at[dp], s3, r3, target=at(partner))
+    for position, plane_z in enumerate(ORDER):
+
+        @pl.when(place < position)
+        def _():
+            pl.semaphore_wait(ready.at[plane_z], 2)
+
+        @pl.when(place != position)
+        def _():
+            for x in range(2):
+                d = x * N_Z + plane_z
+                send(total.at[d], got.at[dp], s3, r3, target=at(d))
+
+    got[dp] = total[dp]
 
     wrow[:, 0:NDOM] = pri[...]
     prior = wrow[...]
@@ -152,7 +186,7 @@
     lane2 = lax.broadcasted_iota(jnp.int32, (N_DP, LANES), 1)
     low = lane2 < HALF
 
-    done(got.at[pl.ds(1, N_DP - 1)], s3, r3, d=1).wait_recv()
+    done(got.at[pl.ds(0, N_DP - 1)], s3, r3, d=1).wait_recv()
     gotf[...] = got[...].astype(f32)
     rank_rows = [gotf[:, r, :] for r in range(RANK)]
     dom0 = jnp.sum(jnp.where(lane2 == COLS, rank_rows[0], 0.0), axis=1, keepdims=True)
@@ -210,9 +244,14 @@
 
     done(part.at[pl.ds(1, N_MP - 1)], s1, r1, m=1).wait_send()
     done(seqbuf, s2, r2, s=1).wait_send()
-    done(got.at[pl.ds(1, N_DP - 1)], s3, r3, d=1).wait_send()
+    done(got.at[pl.ds(0, N_DP - 1)], s3, r3, d=1).wait_send()
     done(rows_a.at[pl.ds(0, len(plane))], s4, r4, s=1).wait_send()
     done(rows_b.at[pl.ds(0, N_DP - 1)], s5, r5, d=1).wait_send()
+
+
+def tail(moved, log_new, out_ref, log_ref):
+    out_ref[...] = moved[...]
+    log_ref[...] = log_new[...]
 
 
 def body(hidden, cotangent, frozen_down, adapter, prior, domain_of):
@@ -248,11 +287,21 @@
             sem((CHUNKS,)),
             sem((3,)),
         ]
-        + [sem] * 10,
+        + [sem] * 10
+        + [pltpu.SemaphoreType.REGULAR((N_Z,))],
         compiler_params=pltpu.CompilerParams(
             collective_id=0, has_side_effects=True, vmem_limit_bytes=60 << 20
         ),
     )(hidden, cotangent, frozen_down.T, adapter.reshape(RANK, COLS), prior.reshape(1, NDOM), domain_of)
+    out, log_new = pl.pallas_call(
+        tail,
+        out_shape=(
+            jax.ShapeDtypeStruct((RANK, COLS), f32),
+            jax.ShapeDtypeStruct((1, NDOM), f32),
+        ),
+        in_specs=[pl.BlockSpec(memory_space=pltpu.VMEM)] * 2,
+        out_specs=(pl.BlockSpec(memory_space=pltpu.VMEM),) * 2,
+    )(out, log_new)
     return out.reshape(1, RANK, COLS), log_new.reshape(NDOM)
 
 

time: 50.4 us -> 46.5 us (0.923)
  local copies, waits for them, and re-layouts: 2.39 us -> 0 us
  Pallas kernels: 47.2 us -> 45.2 us
    pallas_call x1, Pallas kernels: 47.2 us -> 43.9 us  [body(): pl.pallas_call(kernel, out_shape=(jax.ShapeDtypeStruct((RANK, COLS), f32)...]
    unnamed x2 -> x0, local copies, waits for them, and re-layouts: 2.39 us -> none
    pallas_call x0 -> x1, Pallas kernels: none -> 1.25 us  [body(): pl.pallas_call(tail, out_shape=(jax.ShapeDtypeStruct((RANK, COLS), f32),...]
where the time goes in v2:
time: 46.5 us; the launch traced here: 45.8 us
  Pallas kernels  45.2 us (97%)
  between operations  0.64 us (1%)
    pallas_call x1, Pallas kernels, body(): pl.pallas_call(kernel, out_shape=(jax.ShapeDtypeStruct((RANK, COLS), f32)...  43.9 us
    pallas_call x1, Pallas kernels, body(): pl.pallas_call(tail, out_shape=(jax.ShapeDtypeStruct((RANK, COLS), f32),...  1.25 us

profile of v2, /device:TPU:1, one launch (start us, length us, event | category | flops | bytes accessed | tf_op | source)
XLA Modules:
  0.0 45.8 jit_solution(3159515112704380749)
XLA Ops:
  0.6 43.9 %shard_map.77 = (f32[4,35]{1,0:T(4,128)}, f32[1,48]{1,0:T(1,128)}) custom-call(bf16[256,1664]{1,0:T(8,128)(2,1)} %hid_hbm.1, bf16[256,4480]{1,0:T(8,128)(2,1)} %cot_hbm.1, bf16[4,1664]{1,0:T(4,128)(2,1)} %bitcast.5, f32[4,35]{1,0:T(4,128)} %bitcast.6, f32[1,48]{1,0:T(1,128)} %bitcast.7, s32[2]{0:T(128)} %dom_hbm.1), custom_call_target="tpu_custom_call" | custom-call | tf_op jit(solution)/shard_map/pallas_call | solution.py:260
  44.6 1.3 %shard_map.78 = (f32[4,35]{1,0:T(4,128)}, f32[1,48]{1,0:T(1,128)}) custom-call(f32[4,35]{1,0:T(4,128)} %get-tuple-element.6.moved, f32[1,48]{1,0:T(1,128)} %get-tuple-element.7.log_new), custom_call_target="tpu_custom_call" | custom-call | tf_op jit(solution)/shard_map/pallas_call | solution.py:296

commit v3 on v2

--- a/solution.py
+++ b/solution.py
@@ -20,8 +20,9 @@
 COLS = FFM // (N_DP * N_SEQ)
 LANES = 128
 HALF = 64
-CHUNKS = 7
-WIDTH = FFM // CHUNKS
+CHUNKS = 2
+SPAN = N_DP // CHUNKS
+EDGES = tuple(min(c * 2304, FFM) for c in range(CHUNKS + 1))
 
 SEND = jnp.bfloat16
 N_Z = 16
@@ -65,28 +66,34 @@
             device_id=to(**where), device_id_type=MESH,
         )
 
-    barrier = pltpu.get_barrier_semaphore()
-    plane = [(s, m) for s in range(N_SEQ) for m in range(N_MP) if (s, m) != (0, 0)]
-    for s, m in plane:
-        pl.semaphore_signal(barrier, inc=1, device_id=to(s=s, m=m), device_id_type=MESH)
-    pl.semaphore_signal(barrier, inc=1, device_id=to(d=N_Z), device_id_type=MESH)
-    for position, plane_z in enumerate(ORDER):
-
-        @pl.when(place < position)
-        def _():
-            for x in range(2):
-                pl.semaphore_signal(barrier, inc=1, device_id=at(x * N_Z + plane_z), device_id_type=MESH)
-
-
     loads = [
         pltpu.make_async_copy(fro_hbm, fro, in_sem.at[0]),
         pltpu.make_async_copy(hid_hbm, hid, in_sem.at[1]),
     ]
     for load in loads:
         load.start()
+    barrier = pltpu.get_barrier_semaphore()
+    plane = [(s, m) for s in (2, 1, 3, 0) for m in (2, 3, 1, 0) if (s, m) != (0, 0)]
+    near = [(0, m) for m in range(1, N_MP)] + [(s, 0) for s in range(1, N_SEQ)]
+    for s, m in near:
+        pl.semaphore_signal(barrier, inc=1, device_id=to(s=s, m=m), device_id_type=MESH)
+    pl.semaphore_signal(barrier, inc=1, device_id=to(d=N_Z), device_id_type=MESH)
+    for position, plane_z in enumerate(ORDER):
+
+        @pl.when(place < position)
+        def _():
+            for x in range(2):
+                pl.semaphore_signal(barrier, inc=1, device_id=at(x * N_Z + plane_z), device_id_type=MESH)
+
+
+    lhs[...] = jnp.zeros_like(lhs)
+    wrow[...] = jnp.zeros_like(wrow)
+
+    for load in loads:
+        load.wait()
     cot_loads = []
     for c in range(CHUNKS):
-        cut = pl.ds(c * WIDTH, WIDTH)
+        cut = pl.ds(EDGES[c], EDGES[c + 1] - EDGES[c])
         load = pltpu.make_async_copy(cot_hbm.at[:, cut], cot.at[:, cut], cot_sem.at[c])
         load.start()
         cot_loads.append(load)
@@ -98,17 +105,12 @@
     for load in small:
         load.start()
 
-    lhs[...] = jnp.zeros_like(lhs)
-    wrow[...] = jnp.zeros_like(wrow)
-
-    for load in loads:
-        load.wait()
     partial = lax.dot_general(
         fro[...], hid[...], (((1,), (1,)), ((), ())), preferred_element_type=jnp.float32
     )
     part[0] = partial.astype(jnp.bfloat16).astype(jnp.float32)
 
-    pl.semaphore_wait(barrier, len(plane) + 1 + 2 * place)
+    pl.semaphore_wait(barrier, len(near) + 1 + 2 * place)
     for position, plane_z in enumerate(ORDER):
 
         @pl.when(place > position)
@@ -126,30 +128,30 @@
     lhs[0:RANK] = jnp.where(token < PIECE, down, 0.0)
     lhs[8 : 8 + RANK] = jnp.where(token < PIECE, 0.0, down)
     left = lhs[...].astype(jnp.bfloat16)
+    lane = lax.broadcasted_iota(jnp.int32, (8, LANES), 1)
     for c in range(CHUNKS):
-        cut = slice(c * WIDTH, (c + 1) * WIDTH)
+        cut = slice(EDGES[c], EDGES[c + 1])
         cot_loads[c].wait()
         g[:, cut] = jnp.dot(left, cot[:, cut], preferred_element_type=jnp.float32)
-
-    lane = lax.broadcasted_iota(jnp.int32, (8, LANES), 1)
-    for p in range(N_DP * N_SEQ):
-        v, o = divmod(p * COLS, LANES)
-        a = g[0:8, v * LANES : (v + 1) * LANES]
-        b = g[8:16, v * LANES : (v + 1) * LANES]
-        a = a if o == 0 else pltpu.roll(a, LANES - o, 1)
-        b = pltpu.roll(b, (HALF - o) % LANES, 1) if o != HALF else b
-        if o + COLS > LANES:
-            a2 = g[0:8, (v + 1) * LANES : (v + 2) * LANES]
-            b2 = g[8:16, (v + 1) * LANES : (v + 2) * LANES]
-            a2 = pltpu.roll(a2, LANES - o, 1)
-            b2 = pltpu.roll(b2, (HALF - o) % LANES, 1) if o != HALF else b2
-            a = jnp.where(lane < LANES - o, a, a2)
-            b = jnp.where(lane < HALF + LANES - o, b, b2)
-        joined = jnp.where(lane < HALF, a, b)
-        spread[p % N_SEQ, p // N_SEQ] = joined[0:RANK].astype(SEND)
-
-    for s in range(1, N_SEQ):
-        send(spread.at[lax.rem(seq + s, N_SEQ)], seqbuf.at[s - 1], s2, r2, s=s)
+        for p in range(c * SPAN * N_SEQ, (c + 1) * SPAN * N_SEQ):
+            v, o = divmod(p * COLS, LANES)
+            a = g[0:8, v * LANES : (v + 1) * LANES]
+            b = g[8:16, v * LANES : (v + 1) * LANES]
+            a = a if o == 0 else pltpu.roll(a, LANES - o, 1)
+            b = pltpu.roll(b, (HALF - o) % LANES, 1) if o != HALF else b
+            if o + COLS > LANES:
+                a2 = g[0:8, (v + 1) * LANES : (v + 2) * LANES]
+                b2 = g[8:16, (v + 1) * LANES : (v + 2) * LANES]
+                a2 = pltpu.roll(a2, LANES - o, 1)
+                b2 = pltpu.roll(b2, (HALF - o) % LANES, 1) if o != HALF else b2
+                a = jnp.where(lane < LANES - o, a, a2)
+                b = jnp.where(lane < HALF + LANES - o, b, b2)
+            joined = jnp.where(lane < HALF, a, b)
+            spread[p % N_SEQ, p // N_SEQ] = joined[0:RANK].astype(SEND)
+        part_of = pl.ds(c * SPAN, SPAN)
+        for s in (2, 1, 3):
+            send(spread.at[lax.rem(seq + s, N_SEQ), part_of], seqbuf.at[s - 1, part_of], s2, r2, s=s)
+
     for load in small:
         load.wait()
     d0 = dom[0].astype(jnp.float32)
@@ -189,8 +191,8 @@
     done(got.at[pl.ds(0, N_DP - 1)], s3, r3, d=1).wait_recv()
     gotf[...] = got[...].astype(f32)
     rank_rows = [gotf[:, r, :] for r in range(RANK)]
-    dom0 = jnp.sum(jnp.where(lane2 == COLS, rank_rows[0], 0.0), axis=1, keepdims=True)
-    dom1 = jnp.sum(jnp.where(lane2 == HALF + COLS, rank_rows[0], 0.0), axis=1, keepdims=True)
+    dom0 = rank_rows[0][:, COLS : COLS + 1]
+    dom1 = rank_rows[0][:, HALF + COLS : HALF + COLS + 1]
     lanef = lane2.astype(f32)
     hot0 = (lanef == dom0).astype(f32)
     hot1 = (lanef == dom1).astype(f32)
@@ -216,16 +218,17 @@
     row = jnp.sum(hot0 * score0 + hot1 * score1, axis=0, keepdims=True)
     row = jnp.where(lane1 == LANES - 1, sumsq, row)
 
-    mine = seq * N_MP + mp
+    mine = (dp // N_Z * N_SEQ + seq) * N_MP + mp
     rows_a[mine] = row
-    for s, m in plane:
-        send(rows_a.at[mine], rows_a.at[mine], s4, r4, s=s, m=m)
-    done(rows_a.at[pl.ds(0, len(plane))], s4, r4, s=1).wait_recv()
+    slab = [(d, s, m) for s in (2, 1, 3, 0) for d in (N_Z, 0) for m in (2, 3, 1, 0)][:-1]
+    for d, s, m in slab:
+        send(rows_a.at[mine], rows_a.at[mine], s4, r4, d=d, s=s, m=m)
+    done(rows_a.at[pl.ds(0, len(slab))], s4, r4, s=1).wait_recv()
     row = jnp.sum(rows_a[...], axis=0)
-    rows_b[dp] = row
-    for j in range(1, N_DP):
-        send(rows_b.at[dp], rows_b.at[dp], s5, r5, d=j)
-    done(rows_b.at[pl.ds(0, N_DP - 1)], s5, r5, d=1).wait_recv()
+    rows_b[z] = row
+    for j in (8, 7, 9, 6, 10, 5, 11, 4, 12, 3, 13, 2, 14, 1, 15):
+        send(rows_b.at[z], rows_b.at[z], s5, r5, target=at(dp - z + lax.rem(z + j, N_Z)))
+    done(rows_b.at[pl.ds(0, N_Z - 1)], s5, r5, d=1).wait_recv()
     row = jnp.sum(rows_b[...], axis=0)
 
     sumsq = jnp.sum(jnp.where(lane1 == LANES - 1, row, 0.0), axis=1, keepdims=True)
@@ -245,8 +248,8 @@
     done(part.at[pl.ds(1, N_MP - 1)], s1, r1, m=1).wait_send()
     done(seqbuf, s2, r2, s=1).wait_send()
     done(got.at[pl.ds(0, N_DP - 1)], s3, r3, d=1).wait_send()
-    done(rows_a.at[pl.ds(0, len(plane))], s4, r4, s=1).wait_send()
-    done(rows_b.at[pl.ds(0, N_DP - 1)], s5, r5, d=1).wait_send()
+    done(rows_a.at[pl.ds(0, len(slab))], s4, r4, s=1).wait_send()
+    done(rows_b.at[pl.ds(0, N_Z - 1)], s5, r5, d=1).wait_send()
 
 
 def tail(moved, log_new, out_ref, log_ref):
@@ -281,8 +284,8 @@
             pltpu.VMEM((N_DP, RANK, LANES), SEND),
             pltpu.VMEM((N_DP, RANK, LANES), SEND),
             pltpu.VMEM((N_DP, RANK, LANES), f32),
-            pltpu.VMEM((N_SEQ * N_MP, 1, LANES), f32),
-            pltpu.VMEM((N_DP, 1, LANES), f32),
+            pltpu.VMEM((2 * N_SEQ * N_MP, 1, LANES), f32),
+            pltpu.VMEM((N_Z, 1, LANES), f32),
             sem((2,)),
             sem((CHUNKS,)),
             sem((3,)),

time: 46.5 us -> 45.2 us (0.972)
  Pallas kernels: 45.2 us -> 44.3 us
    pallas_call x1, Pallas kernels: 43.9 us -> 43.1 us  [body(): pl.pallas_call(kernel, out_shape=(jax.ShapeDtypeStruct((RANK, COLS), f32)...]
where the time goes in v3:
time: 45.2 us; the launch traced here: 45 us
  Pallas kernels  44.3 us (98%)
  between operations  0.64 us (1%)
    pallas_call x1, Pallas kernels, body(): pl.pallas_call(kernel, out_shape=(jax.ShapeDtypeStruct((RANK, COLS), f32)...  43.1 us
    pallas_call x1, Pallas kernels, body(): pl.pallas_call(tail, out_shape=(jax.ShapeDtypeStruct((RANK, COLS), f32),...  1.25 us

profile of v3, /device:TPU:1, one launch (start us, length us, event | category | flops | bytes accessed | tf_op | source)
XLA Modules:
  0.0 45.0 jit_solution(2631356088118610849)
XLA Ops:
  0.6 43.1 %shard_map.77 = (f32[4,35]{1,0:T(4,128)}, f32[1,48]{1,0:T(1,128)}) custom-call(bf16[256,1664]{1,0:T(8,128)(2,1)} %hid_hbm.1, bf16[256,4480]{1,0:T(8,128)(2,1)} %cot_hbm.1, bf16[4,1664]{1,0:T(4,128)(2,1)} %bitcast.5, f32[4,35]{1,0:T(4,128)} %bitcast.6, f32[1,48]{1,0:T(1,128)} %bitcast.7, s32[2]{0:T(128)} %dom_hbm.1), custom_call_target="tpu_custom_call" | custom-call | tf_op jit(solution)/shard_map/pallas_call | solution.py:263
  43.7 1.3 %shard_map.78 = (f32[4,35]{1,0:T(4,128)}, f32[1,48]{1,0:T(1,128)}) custom-call(f32[4,35]{1,0:T(4,128)} %get-tuple-element.6.moved, f32[1,48]{1,0:T(1,128)} %get-tuple-element.7.log_new), custom_call_target="tpu_custom_call" | custom-call | tf_op jit(solution)/shard_map/pallas_call | solution.py:299

commit v4 on v3

--- a/solution.py
+++ b/solution.py
@@ -26,6 +26,7 @@
 
 SEND = jnp.bfloat16
 N_Z = 16
+SCORERS = (0, 1, 2, 3, 15, 14, 13, 12)
 ORDER = (0, 1, 2, 3, 4, 5, 6, 7, 15, 8, 14, 9, 13, 10, 12, 11)
 MESH = pl.DeviceIdType.MESH
 step_rate = 1.0
@@ -36,7 +37,7 @@
     hid_hbm, cot_hbm, fro_hbm, ada_hbm, pri_hbm, dom_hbm,
     out_ref, log_ref,
     hid, cot, fro, ada, pri, dom, wrow, part, lhs, g, spread, seqbuf, total, got, gotf, rows_a, rows_b,
-    in_sem, cot_sem, small_sem, s1, r1, s2, r2, s3, r3, s4, r4, s5, r5, ready,
+    in_sem, cot_sem, small_sem, s1, r1, s2, r2, s3, r3, s4, r4, s5, r5, s6, r6, ready,
 ):
     dp, seq, mp = lax.axis_index("dp"), lax.axis_index("seq"), lax.axis_index("mp")
 
@@ -49,6 +50,9 @@
 
     z = lax.rem(dp, N_Z)
     place = jnp.where(z < 8, z, jnp.where(z < 12, 2 * z - 7, 38 - 2 * z))
+
+    scorer = (z < 4) | (z >= 12)
+    second = jnp.where(z < 4, z + 4, z - 4)
 
     def at(d):
         return {"dp": d, "seq": seq, "mp": mp}
@@ -165,9 +169,8 @@
     summed = jnp.where(lane3 == COLS, d0, jnp.where(lane3 == HALF + COLS, d1, summed))
     total[...] = summed.astype(SEND)
 
-    partner = lax.rem(dp + N_Z, N_DP)
-    send(total.at[partner], got.at[dp], s3, r3, target=at(partner))
-    for position, plane_z in enumerate(ORDER):
+    def exchange(plane_z, scored):
+        position = ORDER.index(plane_z)
 
         @pl.when(place < position)
         def _():
@@ -177,9 +180,26 @@
         def _():
             for x in range(2):
                 d = x * N_Z + plane_z
-                send(total.at[d], got.at[dp], s3, r3, target=at(d))
-
-    got[dp] = total[dp]
+                if scored:
+                    other = d + 4 if plane_z < 4 else d - 4
+                    send(total.at[other], got.at[1, dp], s6, r6, target=at(d))
+                send(total.at[d], got.at[0, dp], s3, r3, target=at(d))
+
+    base = dp - z
+    partner = lax.rem(dp + N_Z, N_DP)
+    for plane_z in SCORERS:
+        exchange(plane_z, True)
+
+    @pl.when(scorer)
+    def _():
+        send(total.at[partner - z + second], got.at[1, dp], s6, r6, target=at(partner))
+        got[1, dp] = total[base + second]
+
+    send(total.at[partner], got.at[0, dp], s3, r3, target=at(partner))
+    got[0, dp] = total[dp]
+    for plane_z in ORDER:
+        if plane_z not in SCORERS:
+            exchange(plane_z, False)
 
     wrow[:, 0:NDOM] = pri[...]
     prior = wrow[...]
@@ -188,9 +208,9 @@
     lane2 = lax.broadcasted_iota(jnp.int32, (N_DP, LANES), 1)
     low = lane2 < HALF
 
-    done(got.at[pl.ds(0, N_DP - 1)], s3, r3, d=1).wait_recv()
-    gotf[...] = got[...].astype(f32)
-    rank_rows = [gotf[:, r, :] for r in range(RANK)]
+    done(got.at[0, pl.ds(0, N_DP - 1)], s3, r3, d=1).wait_recv()
+    gotf[0] = got[0].astype(f32)
+    rank_rows = [gotf[0, :, r, :] for r in range(RANK)]
     dom0 = rank_rows[0][:, COLS : COLS + 1]
     dom1 = rank_rows[0][:, HALF + COLS : HALF + COLS + 1]
     lanef = lane2.astype(f32)
@@ -204,31 +224,52 @@
             jnp.sum(hot1 * row, axis=1, keepdims=True),
         )
 
-    def combine(scale):
-        sums = [jnp.sum(scale * x, axis=0, keepdims=True) for x in rank_rows]
+    def combine(scale, block):
+        sums = [jnp.sum(scale * x, axis=0, keepdims=True) for x in block]
         return [x + pltpu.roll(x, HALF, 1) for x in sums]
 
-    valid = (lane1 < COLS) | ((lane1 >= HALF) & (lane1 < HALF + COLS))
-    mixture = [jnp.where(valid, x, 0.0) for x in combine(per_sequence(weights))]
-    square = sum(x * x for x in mixture)
-    sumsq = jnp.sum(jnp.where(lane1 < HALF, square, 0.0), axis=1, keepdims=True)
-    product = sum(x * y for x, y in zip(rank_rows, mixture))
-    score0 = jnp.sum(jnp.where(low, product, 0.0), axis=1, keepdims=True)
-    score1 = jnp.sum(jnp.where(low, 0.0, product), axis=1, keepdims=True)
-    row = jnp.sum(hot0 * score0 + hot1 * score1, axis=0, keepdims=True)
-    row = jnp.where(lane1 == LANES - 1, sumsq, row)
-
-    mine = (dp // N_Z * N_SEQ + seq) * N_MP + mp
-    rows_a[mine] = row
-    slab = [(d, s, m) for s in (2, 1, 3, 0) for d in (N_Z, 0) for m in (2, 3, 1, 0)][:-1]
-    for d, s, m in slab:
-        send(rows_a.at[mine], rows_a.at[mine], s4, r4, d=d, s=s, m=m)
-    done(rows_a.at[pl.ds(0, len(slab))], s4, r4, s=1).wait_recv()
-    row = jnp.sum(rows_a[...], axis=0)
-    rows_b[z] = row
-    for j in (8, 7, 9, 6, 10, 5, 11, 4, 12, 3, 13, 2, 14, 1, 15):
-        send(rows_b.at[z], rows_b.at[z], s5, r5, target=at(dp - z + lax.rem(z + j, N_Z)))
-    done(rows_b.at[pl.ds(0, N_Z - 1)], s5, r5, d=1).wait_recv()
+    @pl.when(scorer)
+    def _():
+        done(got.at[1, pl.ds(0, N_DP - 1)], s6, r6, d=1).wait_recv()
+        gotf[1] = got[1].astype(f32)
+        second_rows = [gotf[1, :, r, :] for r in range(RANK)]
+        valid = (lane1 < COLS) | ((lane1 >= HALF) & (lane1 < HALF + COLS))
+        mine_w = per_sequence(weights)
+        square = jnp.zeros((1, LANES), f32)
+        product = jnp.zeros((N_DP, LANES), f32)
+        for block in (rank_rows, second_rows):
+            mixture = [jnp.where(valid, x, 0.0) for x in combine(mine_w, block)]
+            square += sum(x * x for x in mixture)
+            product += sum(x * y for x, y in zip(block, mixture))
+        sumsq = jnp.sum(jnp.where(lane1 < HALF, square, 0.0), axis=1, keepdims=True)
+        score0 = jnp.sum(jnp.where(low, product, 0.0), axis=1, keepdims=True)
+        score1 = jnp.sum(jnp.where(low, 0.0, product), axis=1, keepdims=True)
+        row = jnp.sum(hot0 * score0 + hot1 * score1, axis=0, keepdims=True)
+        row = jnp.where(lane1 == LANES - 1, sumsq, row)
+        mine = (dp // N_Z * N_SEQ + seq) * N_MP + mp
+        rows_a[mine] = row
+        slab = [(d, s, m) for s in (2, 1, 3, 0) for d in (N_Z, 0) for m in (2, 3, 1, 0)][:-1]
+        for d, s, m in slab:
+            send(rows_a.at[mine], rows_a.at[mine], s4, r4, d=d, s=s, m=m)
+        done(rows_a.at[pl.ds(0, len(slab))], s4, r4, s=1).wait_recv()
+        slot = jnp.where(z < 4, z, z - 8)
+        rows_b[slot] = jnp.sum(rows_a[...], axis=0)
+        for plane_z in (0, 1, 2, 3, 4, 5, 6, 7, 8, 15, 14, 9, 13, 10, 12, 11):
+
+            @pl.when(z != plane_z)
+            def _():
+                send(rows_b.at[slot], rows_b.at[slot], s5, r5, target=at(base + plane_z))
+
+        done(rows_b.at[pl.ds(0, len(SCORERS) - 1)], s5, r5, d=1).wait_recv()
+        done(rows_a.at[pl.ds(0, len(slab))], s4, r4, s=1).wait_send()
+        done(rows_a.at[pl.ds(0, N_Z - 1)], s5, r5, d=1).wait_send()
+        done(got.at[1, pl.ds(0, len(SCORERS) * 2 - 1)], s6, r6, d=1).wait_send()
+
+    @pl.when(jnp.logical_not(scorer))
+    def _():
+        done(rows_b, s5, r5, d=1).wait_recv()
+        done(got.at[1, pl.ds(0, len(SCORERS) * 2)], s6, r6, d=1).wait_send()
+
     row = jnp.sum(rows_b[...], axis=0)
 
     sumsq = jnp.sum(jnp.where(lane1 == LANES - 1, row, 0.0), axis=1, keepdims=True)
@@ -239,7 +280,7 @@
     log_new = jnp.log(weights) + step_rate * ratio - jnp.log(jnp.sum(raised, axis=1, keepdims=True))
     log_ref[...] = log_new[:, 0:NDOM]
     new = jnp.where(lane1 < NDOM, jnp.exp(log_new), 0.0)
-    update = combine(per_sequence(new))
+    update = combine(per_sequence(new), rank_rows)
     root = jnp.sqrt(meansq)
     for r in range(RANK):
         moved = learn_rate * update[r] / root
@@ -247,9 +288,7 @@
 
     done(part.at[pl.ds(1, N_MP - 1)], s1, r1, m=1).wait_send()
     done(seqbuf, s2, r2, s=1).wait_send()
-    done(got.at[pl.ds(0, N_DP - 1)], s3, r3, d=1).wait_send()
-    done(rows_a.at[pl.ds(0, len(slab))], s4, r4, s=1).wait_send()
-    done(rows_b.at[pl.ds(0, N_Z - 1)], s5, r5, d=1).wait_send()
+    done(got.at[0, pl.ds(0, N_DP - 1)], s3, r3, d=1).wait_send()
 
 
 def tail(moved, log_new, out_ref, log_ref):
@@ -282,15 +321,15 @@
             pltpu.VMEM((N_SEQ, N_DP, RANK, LANES), SEND),
             pltpu.VMEM((N_SEQ - 1, N_DP, RANK, LANES), SEND),
             pltpu.VMEM((N_DP, RANK, LANES), SEND),
-            pltpu.VMEM((N_DP, RANK, LANES), SEND),
-            pltpu.VMEM((N_DP, RANK, LANES), f32),
+            pltpu.VMEM((2, N_DP, RANK, LANES), SEND),
+            pltpu.VMEM((2, N_DP, RANK, LANES), f32),
             pltpu.VMEM((2 * N_SEQ * N_MP, 1, LANES), f32),
-            pltpu.VMEM((N_Z, 1, LANES), f32),
+            pltpu.VMEM((len(SCORERS), 1, LANES), f32),
             sem((2,)),
             sem((CHUNKS,)),
             sem((3,)),
         ]
-        + [sem] * 10
+        + [sem] * 12
         + [pltpu.SemaphoreType.REGULAR((N_Z,))],
         compiler_params=pltpu.CompilerParams(
             collective_id=0, has_side_effects=True, vmem_limit_bytes=60 << 20

time: 45.2 us -> 41.9 us (0.927)
  Pallas kernels: 44.3 us -> 41 us
    pallas_call x1, Pallas kernels: 43.1 us -> 39.8 us  [body(): pl.pallas_call(kernel, out_shape=(jax.ShapeDtypeStruct((RANK, COLS), f32)...]
where the time goes in v4:
time: 41.9 us; the launch traced here: 41.7 us
  Pallas kernels  41 us (98%)
  between operations  0.64 us (2%)
    pallas_call x1, Pallas kernels, body(): pl.pallas_call(kernel, out_shape=(jax.ShapeDtypeStruct((RANK, COLS), f32)...  39.8 us
    pallas_call x1, Pallas kernels, body(): pl.pallas_call(tail, out_shape=(jax.ShapeDtypeStruct((RANK, COLS), f32),...  1.25 us

profile of v4, /device:TPU:1, one launch (start us, length us, event | category | flops | bytes accessed | tf_op | source)
XLA Modules:
  0.0 41.7 jit_solution(3348891945672234027)
XLA Ops:
  0.6 39.8 %shard_map.77 = (f32[4,35]{1,0:T(4,128)}, f32[1,48]{1,0:T(1,128)}) custom-call(bf16[256,1664]{1,0:T(8,128)(2,1)} %hid_hbm.1, bf16[256,4480]{1,0:T(8,128)(2,1)} %cot_hbm.1, bf16[4,1664]{1,0:T(4,128)(2,1)} %bitcast.5, f32[4,35]{1,0:T(4,128)} %bitcast.6, f32[1,48]{1,0:T(1,128)} %bitcast.7, s32[2]{0:T(128)} %dom_hbm.1), custom_call_target="tpu_custom_call" | custom-call | tf_op jit(solution)/shard_map/pallas_call | solution.py:302
  40.4 1.3 %shard_map.78 = (f32[4,35]{1,0:T(4,128)}, f32[1,48]{1,0:T(1,128)}) custom-call(f32[4,35]{1,0:T(4,128)} %get-tuple-element.6.moved, f32[1,48]{1,0:T(1,128)} %get-tuple-element.7.log_new), custom_call_target="tpu_custom_call" | custom-call | tf_op jit(solution)/shard_map/pallas_call | solution.py:338

commit v5 on v4

--- a/solution.py
+++ b/solution.py
@@ -26,6 +26,8 @@
 
 SEND = jnp.bfloat16
 N_Z = 16
+SIDE = 4
+BLOCKS = N_Z // (2 * SIDE)
 SCORERS = (0, 1, 2, 3, 15, 14, 13, 12)
 ORDER = (0, 1, 2, 3, 4, 5, 6, 7, 15, 8, 14, 9, 13, 10, 12, 11)
 MESH = pl.DeviceIdType.MESH
@@ -51,8 +53,8 @@
     z = lax.rem(dp, N_Z)
     place = jnp.where(z < 8, z, jnp.where(z < 12, 2 * z - 7, 38 - 2 * z))
 
-    scorer = (z < 4) | (z >= 12)
-    second = jnp.where(z < 4, z + 4, z - 4)
+    scorer = (z < SIDE) | (z >= N_Z - SIDE)
+    stride = jnp.where(z < SIDE, SIDE, -SIDE)
 
     def at(d):
         return {"dp": d, "seq": seq, "mp": mp}
@@ -181,8 +183,9 @@
             for x in range(2):
                 d = x * N_Z + plane_z
                 if scored:
-                    other = d + 4 if plane_z < 4 else d - 4
-                    send(total.at[other], got.at[1, dp], s6, r6, target=at(d))
+                    step = SIDE if plane_z < SIDE else -SIDE
+                    for k in range(1, BLOCKS):
+                        send(total.at[d + k * step], got.at[k, dp], s6, r6, target=at(d))
                 send(total.at[d], got.at[0, dp], s3, r3, target=at(d))
 
     base = dp - z
@@ -192,15 +195,18 @@
 
     @pl.when(scorer)
     def _():
-        send(total.at[partner - z + second], got.at[1, dp], s6, r6, target=at(partner))
-        got[1, dp] = total[base + second]
+        for k in range(1, BLOCKS):
+            send(total.at[partner + k * stride], got.at[k, dp], s6, r6, target=at(partner))
+            got[k, dp] = total[dp + k * stride]
 
     send(total.at[partner], got.at[0, dp], s3, r3, target=at(partner))
     got[0, dp] = total[dp]
-    for plane_z in ORDER:
-        if plane_z not in SCORERS:
-            exchange(plane_z, False)
-
+    def rest():
+        for plane_z in ORDER:
+            if plane_z not in SCORERS:
+                exchange(plane_z, False)
+
+    pl.when(jnp.logical_not(scorer))(rest)
     wrow[:, 0:NDOM] = pri[...]
     prior = wrow[...]
     weights = prior / jnp.sum(prior, axis=1, keepdims=True)
@@ -230,14 +236,17 @@
 
     @pl.when(scorer)
     def _():
-        done(got.at[1, pl.ds(0, N_DP - 1)], s6, r6, d=1).wait_recv()
-        gotf[1] = got[1].astype(f32)
-        second_rows = [gotf[1, :, r, :] for r in range(RANK)]
+        others = got.at[pl.ds(1, BLOCKS - 1), pl.ds(0, N_DP - 1)]
+        done(others, s6, r6, d=1).wait_recv()
+        blocks = [rank_rows]
+        for k in range(1, BLOCKS):
+            gotf[k] = got[k].astype(f32)
+            blocks.append([gotf[k, :, r, :] for r in range(RANK)])
         valid = (lane1 < COLS) | ((lane1 >= HALF) & (lane1 < HALF + COLS))
         mine_w = per_sequence(weights)
         square = jnp.zeros((1, LANES), f32)
         product = jnp.zeros((N_DP, LANES), f32)
-        for block in (rank_rows, second_rows):
+        for block in blocks:
             mixture = [jnp.where(valid, x, 0.0) for x in combine(mine_w, block)]
             square += sum(x * x for x in mixture)
             product += sum(x * y for x, y in zip(block, mixture))
@@ -252,7 +261,7 @@
         for d, s, m in slab:
             send(rows_a.at[mine], rows_a.at[mine], s4, r4, d=d, s=s, m=m)
         done(rows_a.at[pl.ds(0, len(slab))], s4, r4, s=1).wait_recv()
-        slot = jnp.where(z < 4, z, z - 8)
+        slot = jnp.where(z < SIDE, z, z - (N_Z - 2 * SIDE))
         rows_b[slot] = jnp.sum(rows_a[...], axis=0)
         for plane_z in (0, 1, 2, 3, 4, 5, 6, 7, 8, 15, 14, 9, 13, 10, 12, 11):
 
@@ -260,15 +269,18 @@
             def _():
                 send(rows_b.at[slot], rows_b.at[slot], s5, r5, target=at(base + plane_z))
 
+        rest()
         done(rows_b.at[pl.ds(0, len(SCORERS) - 1)], s5, r5, d=1).wait_recv()
         done(rows_a.at[pl.ds(0, len(slab))], s4, r4, s=1).wait_send()
         done(rows_a.at[pl.ds(0, N_Z - 1)], s5, r5, d=1).wait_send()
-        done(got.at[1, pl.ds(0, len(SCORERS) * 2 - 1)], s6, r6, d=1).wait_send()
+        sent = got.at[pl.ds(1, BLOCKS - 1), pl.ds(0, len(SCORERS) * 2 - 1)]
+        done(sent, s6, r6, d=1).wait_send()
 
     @pl.when(jnp.logical_not(scorer))
     def _():
         done(rows_b, s5, r5, d=1).wait_recv()
-        done(got.at[1, pl.ds(0, len(SCORERS) * 2)], s6, r6, d=1).wait_send()
+        sent = got.at[pl.ds(1, BLOCKS - 1), pl.ds(0, len(SCORERS) * 2)]
+        done(sent, s6, r6, d=1).wait_send()
 
     row = jnp.sum(rows_b[...], axis=0)
 
@@ -321,8 +333,8 @@
             pltpu.VMEM((N_SEQ, N_DP, RANK, LANES), SEND),
             pltpu.VMEM((N_SEQ - 1, N_DP, RANK, LANES), SEND),
             pltpu.VMEM((N_DP, RANK, LANES), SEND),
-            pltpu.VMEM((2, N_DP, RANK, LANES), SEND),
-            pltpu.VMEM((2, N_DP, RANK, LANES), f32),
+            pltpu.VMEM((BLOCKS, N_DP, RANK, LANES), SEND),
+            pltpu.VMEM((BLOCKS, N_DP, RANK, LANES), f32),
             pltpu.VMEM((2 * N_SEQ * N_MP, 1, LANES), f32),
             pltpu.VMEM((len(SCORERS), 1, LANES), f32),
             sem((2,)),

time: 41.9 us -> 41.8 us (level)
  no operation moved by 1% of the time
where the time goes in v5:
time: 41.8 us; the launch traced here: 41.6 us
  Pallas kernels  40.9 us (98%)
  between operations  0.64 us (2%)
    pallas_call x1, Pallas kernels, body(): pl.pallas_call(kernel, out_shape=(jax.ShapeDtypeStruct((RANK, COLS), f32)...  39.7 us
    pallas_call x1, Pallas kernels, body(): pl.pallas_call(tail, out_shape=(jax.ShapeDtypeStruct((RANK, COLS), f32),...  1.25 us

profile of v5, /device:TPU:1, one launch (start us, length us, event | category | flops | bytes accessed | tf_op | source)
XLA Modules:
  0.0 41.6 jit_solution(4734864384421299298)
XLA Ops:
  0.6 39.7 %shard_map.77 = (f32[4,35]{1,0:T(4,128)}, f32[1,48]{1,0:T(1,128)}) custom-call(bf16[256,1664]{1,0:T(8,128)(2,1)} %hid_hbm.1, bf16[256,4480]{1,0:T(8,128)(2,1)} %cot_hbm.1, bf16[4,1664]{1,0:T(4,128)(2,1)} %bitcast.5, f32[4,35]{1,0:T(4,128)} %bitcast.6, f32[1,48]{1,0:T(1,128)} %bitcast.7, s32[2]{0:T(128)} %dom_hbm.1), custom_call_target="tpu_custom_call" | custom-call | tf_op jit(solution)/shard_map/pallas_call | solution.py:314
  40.3 1.3 %shard_map.78 = (f32[4,35]{1,0:T(4,128)}, f32[1,48]{1,0:T(1,128)}) custom-call(f32[4,35]{1,0:T(4,128)} %get-tuple-element.6.moved, f32[1,48]{1,0:T(1,128)} %get-tuple-element.7.log_new), custom_call_target="tpu_custom_call" | custom-call | tf_op jit(solution)/shard_map/pallas_call | solution.py:350

commit v6 on v5

--- a/solution.py
+++ b/solution.py
@@ -26,9 +26,11 @@
 
 SEND = jnp.bfloat16
 N_Z = 16
-SIDE = 4
+SIDE = 2
+EARLY = 4
+SLAB = 32
 BLOCKS = N_Z // (2 * SIDE)
-SCORERS = (0, 1, 2, 3, 15, 14, 13, 12)
+SCORERS = (0, 1, 15, 14)
 ORDER = (0, 1, 2, 3, 4, 5, 6, 7, 15, 8, 14, 9, 13, 10, 12, 11)
 MESH = pl.DeviceIdType.MESH
 step_rate = 1.0
@@ -255,34 +257,54 @@
         score1 = jnp.sum(jnp.where(low, 0.0, product), axis=1, keepdims=True)
         row = jnp.sum(hot0 * score0 + hot1 * score1, axis=0, keepdims=True)
         row = jnp.where(lane1 == LANES - 1, sumsq, row)
-        mine = (dp // N_Z * N_SEQ + seq) * N_MP + mp
+        slot = jnp.where(z < SIDE, z, z - (N_Z - 2 * SIDE))
+        mine = ((slot * 2 + dp // N_Z) * N_SEQ + seq) * N_MP + mp
         rows_a[mine] = row
-        slab = [(d, s, m) for s in (2, 1, 3, 0) for d in (N_Z, 0) for m in (2, 3, 1, 0)][:-1]
-        for d, s, m in slab:
-            send(rows_a.at[mine], rows_a.at[mine], s4, r4, d=d, s=s, m=m)
-        done(rows_a.at[pl.ds(0, len(slab))], s4, r4, s=1).wait_recv()
-        slot = jnp.where(z < SIDE, z, z - (N_Z - 2 * SIDE))
-        rows_b[slot] = jnp.sum(rows_a[...], axis=0)
-        for plane_z in (0, 1, 2, 3, 4, 5, 6, 7, 8, 15, 14, 9, 13, 10, 12, 11):
-
-            @pl.when(z != plane_z)
-            def _():
-                send(rows_b.at[slot], rows_b.at[slot], s5, r5, target=at(base + plane_z))
+        slab = [(d, s, m) for s in (2, 1, 3, 0) for d in (1, 0) for m in (2, 3, 1, 0)]
+
+        @pl.loop(0, EARLY)
+        def _(plane_z):
+            for d, s, m in slab:
+                target = {
+                    "dp": lax.rem(dp // N_Z + d, 2) * N_Z + plane_z,
+                    "seq": lax.rem(seq + s, N_SEQ),
+                    "mp": lax.rem(mp + m, N_MP),
+                }
+
+                def push(target=target):
+                    send(rows_a.at[mine], rows_a.at[mine], s4, r4, target=target)
+
+                if (d, s, m) == (0, 0, 0):
+                    pl.when(z != plane_z)(push)
+                else:
+                    push()
 
         rest()
-        done(rows_b.at[pl.ds(0, len(SCORERS) - 1)], s5, r5, d=1).wait_recv()
-        done(rows_a.at[pl.ds(0, len(slab))], s4, r4, s=1).wait_send()
-        done(rows_a.at[pl.ds(0, N_Z - 1)], s5, r5, d=1).wait_send()
-        sent = got.at[pl.ds(1, BLOCKS - 1), pl.ds(0, len(SCORERS) * 2 - 1)]
-        done(sent, s6, r6, d=1).wait_send()
-
-    @pl.when(jnp.logical_not(scorer))
-    def _():
-        done(rows_b, s5, r5, d=1).wait_recv()
-        sent = got.at[pl.ds(1, BLOCKS - 1), pl.ds(0, len(SCORERS) * 2)]
-        done(sent, s6, r6, d=1).wait_send()
-
-    row = jnp.sum(rows_b[...], axis=0)
+
+    rows_in = 2 * SIDE * SLAB
+
+    @pl.when(z < EARLY)
+    def _():
+        @pl.when(scorer)
+        def _():
+            done(rows_a.at[pl.ds(0, rows_in - 1)], s4, r4, d=1).wait_recv()
+
+        @pl.when(jnp.logical_not(scorer))
+        def _():
+            done(rows_a, s4, r4, d=1).wait_recv()
+
+        rows_b[0] = jnp.sum(rows_a[...], axis=0)
+
+        @pl.when(z == 0)
+        def _():
+            for plane_z in (8, 7, 9, 6, 10, 5, 11, 4, 12, 13, 14, 15):
+                send(rows_b.at[0], rows_b.at[0], s5, r5, target=at(base + plane_z))
+
+    @pl.when(z >= EARLY)
+    def _():
+        done(rows_b.at[pl.ds(0, 1)], s5, r5, d=1).wait_recv()
+
+    row = rows_b[0]
 
     sumsq = jnp.sum(jnp.where(lane1 == LANES - 1, row, 0.0), axis=1, keepdims=True)
     scores = jnp.where(lane1 < NDOM, row, 0.0)
@@ -297,6 +319,30 @@
     for r in range(RANK):
         moved = learn_rate * update[r] / root
         out_ref[r : r + 1, :] = ada[r : r + 1, :] - moved[:, 0:COLS]
+
+    @pl.when(scorer)
+    def _():
+        done(rows_a.at[pl.ds(0, 2 * SLAB)], s4, r4, d=1).wait_send()
+
+        @pl.when(z < EARLY)
+        def _():
+            done(rows_a.at[pl.ds(0, 2 * SLAB - 1)], s4, r4, d=1).wait_send()
+
+        @pl.when(z >= EARLY)
+        def _():
+            done(rows_a.at[pl.ds(0, 2 * SLAB)], s4, r4, d=1).wait_send()
+
+        sent = got.at[pl.ds(1, BLOCKS - 1), pl.ds(0, len(SCORERS) * 2 - 1)]
+        done(sent, s6, r6, d=1).wait_send()
+
+    @pl.when(jnp.logical_not(scorer))
+    def _():
+        sent = got.at[pl.ds(1, BLOCKS - 1), pl.ds(0, len(SCORERS) * 2)]
+        done(sent, s6, r6, d=1).wait_send()
+
+    @pl.when(z == 0)
+    def _():
+        done(rows_a.at[pl.ds(0, N_Z - EARLY)], s5, r5, d=1).wait_send()
 
     done(part.at[pl.ds(1, N_MP - 1)], s1, r1, m=1).wait_send()
     done(seqbuf, s2, r2, s=1).wait_send()
@@ -335,8 +381,8 @@
             pltpu.VMEM((N_DP, RANK, LANES), SEND),
             pltpu.VMEM((BLOCKS, N_DP, RANK, LANES), SEND),
             pltpu.VMEM((BLOCKS, N_DP, RANK, LANES), f32),
-            pltpu.VMEM((2 * N_SEQ * N_MP, 1, LANES), f32),
-            pltpu.VMEM((len(SCORERS), 1, LANES), f32),
+            pltpu.VMEM((2 * SIDE * SLAB, 1, LANES), f32),
+            pltpu.VMEM((1, 1, LANES), f32),
             sem((2,)),
             sem((CHUNKS,)),
             sem((3,)),

time: 41.8 us -> 41.2 us (0.986)
  Pallas kernels: 40.9 us -> 40.3 us
    pallas_call x1, Pallas kernels: 39.7 us -> 39.1 us  [body(): pl.pallas_call(kernel, out_shape=(jax.ShapeDtypeStruct((RANK, COLS), f32)...]
where the time goes in v6:
time: 41.2 us; the launch traced here: 41 us
  Pallas kernels  40.3 us (98%)
  between operations  0.64 us (2%)
    pallas_call x1, Pallas kernels, body(): pl.pallas_call(kernel, out_shape=(jax.ShapeDtypeStruct((RANK, COLS), f32)...  39.1 us
    pallas_call x1, Pallas kernels, body(): pl.pallas_call(tail, out_shape=(jax.ShapeDtypeStruct((RANK, COLS), f32),...  1.25 us

profile of v6, /device:TPU:1, one launch (start us, length us, event | category | flops | bytes accessed | tf_op | source)
XLA Modules:
  0.0 41.0 jit_solution(7267854587780253994)
XLA Ops:
  0.6 39.1 %shard_map.77 = (f32[4,35]{1,0:T(4,128)}, f32[1,48]{1,0:T(1,128)}) custom-call(bf16[256,1664]{1,0:T(8,128)(2,1)} %hid_hbm.1, bf16[256,4480]{1,0:T(8,128)(2,1)} %cot_hbm.1, bf16[4,1664]{1,0:T(4,128)(2,1)} %bitcast.5, f32[4,35]{1,0:T(4,128)} %bitcast.6, f32[1,48]{1,0:T(1,128)} %bitcast.7, s32[2]{0:T(128)} %dom_hbm.1), custom_call_target="tpu_custom_call" | custom-call | tf_op jit(solution)/shard_map/pallas_call | solution.py:360
  39.7 1.3 %shard_map.78 = (f32[4,35]{1,0:T(4,128)}, f32[1,48]{1,0:T(1,128)}) custom-call(f32[4,35]{1,0:T(4,128)} %get-tuple-element.6.moved, f32[1,48]{1,0:T(1,128)} %get-tuple-element.7.log_new), custom_call_target="tpu_custom_call" | custom-call | tf_op jit(solution)/shard_map/pallas_call | solution.py:396

commit v7 on v6

--- a/solution.py
+++ b/solution.py
@@ -27,7 +27,7 @@
 SEND = jnp.bfloat16
 N_Z = 16
 SIDE = 2
-EARLY = 4
+EARLY = 3
 SLAB = 32
 BLOCKS = N_Z // (2 * SIDE)
 SCORERS = (0, 1, 15, 14)
@@ -297,7 +297,7 @@
 
         @pl.when(z == 0)
         def _():
-            for plane_z in (8, 7, 9, 6, 10, 5, 11, 4, 12, 13, 14, 15):
+            for plane_z in (3, 4, 8, 5, 7, 6, 9, 10, 11, 12, 13, 14, 15):
                 send(rows_b.at[0], rows_b.at[0], s5, r5, target=at(base + plane_z))
 
     @pl.when(z >= EARLY)
@@ -322,7 +322,7 @@
 
     @pl.when(scorer)
     def _():
-        done(rows_a.at[pl.ds(0, 2 * SLAB)], s4, r4, d=1).wait_send()
+        done(rows_a.at[pl.ds(0, SLAB)], s4, r4, d=1).wait_send()
 
         @pl.when(z < EARLY)
         def _():

time: 41.2 us -> 41.2 us (level)
  no operation moved by 1% of the time
where the time goes in v7:
time: 41.2 us; the launch traced here: 41 us
  Pallas kernels  40.3 us (98%)
  between operations  0.64 us (2%)
    pallas_call x1, Pallas kernels, body(): pl.pallas_call(kernel, out_shape=(jax.ShapeDtypeStruct((RANK, COLS), f32)...  39.1 us
    pallas_call x1, Pallas kernels, body(): pl.pallas_call(tail, out_shape=(jax.ShapeDtypeStruct((RANK, COLS), f32),...  1.25 us

profile of v7, /device:TPU:1, one launch (start us, length us, event | category | flops | bytes accessed | tf_op | source)
XLA Modules:
  0.0 41.0 jit_solution(4475788522007168414)
XLA Ops:
  0.6 39.1 %shard_map.77 = (f32[4,35]{1,0:T(4,128)}, f32[1,48]{1,0:T(1,128)}) custom-call(bf16[256,1664]{1,0:T(8,128)(2,1)} %hid_hbm.1, bf16[256,4480]{1,0:T(8,128)(2,1)} %cot_hbm.1, bf16[4,1664]{1,0:T(4,128)(2,1)} %bitcast.5, f32[4,35]{1,0:T(4,128)} %bitcast.6, f32[1,48]{1,0:T(1,128)} %bitcast.7, s32[2]{0:T(128)} %dom_hbm.1), custom_call_target="tpu_custom_call" | custom-call | tf_op jit(solution)/shard_map/pallas_call | solution.py:360
  39.7 1.3 %shard_map.78 = (f32[4,35]{1,0:T(4,128)}, f32[1,48]{1,0:T(1,128)}) custom-call(f32[4,35]{1,0:T(4,128)} %get-tuple-element.6.moved, f32[1,48]{1,0:T(1,128)} %get-tuple-element.7.log_new), custom_call_target="tpu_custom_call" | custom-call | tf_op jit(solution)/shard_map/pallas_call | solution.py:396
